TPU v7x, 32 devices: a whole 2x2x4 slice. The times are simulated.
32 devices in a mesh: dp: 8 (over z, y), tensor: 4 (over x, core).
Axes of the slice: x: 2, y: 2, z: 4, core: 2. Of those that a mesh axis runs over, the one named last changes fastest.
Arguments:
- tokens: bfloat16 [16384, 768], P(('dp', 'tensor'))
- first_values: bfloat16 [16384, 384], P(('dp', 'tensor')), may hold values from -6 to 6
- pieces: int32 [16384], P('dp'), may hold values from 0 to 64, as said below
- lengths: int32 [8], P('dp'), may hold values from 256 to 2048, as said below
- w_query: bfloat16 [768, 768], P('dp', 'tensor'), may hold values from -0.21875 to 0.21875
- w_key: bfloat16 [768, 768], P('dp', 'tensor'), may hold values from -0.21875 to 0.21875
- w_value: bfloat16 [768, 384], P('dp'), may hold values from -0.21875 to 0.21875
- w_out: bfloat16 [768, 768], P('tensor', 'dp'), may hold values from -2.5 to 2.5
- w_up: bfloat16 [768, 3072], P('dp', 'tensor'), may hold values from -0.21875 to 0.21875
- w_down: bfloat16 [3072, 768], P('tensor', 'dp'), may hold values from -0.15625 to 0.15625
- gain_attn: float32 [768], replicated, may hold values from 0.1 to 1.9
- gain_mlp: float32 [768], replicated, may hold values from 0.1 to 1.9
- cotangent: bfloat16 [16384, 768], P(('dp', 'tensor')), may hold values from -6 to 6
Outputs:
- output: bfloat16 [16384, 768], P(('dp', 'tensor'))
- d_tokens: float32 [16384, 768], P(('dp', 'tensor'))
- d_first_values: float32 [16384, 384], P(('dp', 'tensor'))
- d_w_query: float32 [768, 768], P('dp', 'tensor')
- d_w_key: float32 [768, 768], P('dp', 'tensor')
- d_w_value: float32 [768, 384], P('dp')
- d_w_out: float32 [768, 768], P('tensor', 'dp')
- d_w_up: float32 [768, 3072], P('dp', 'tensor')
- d_w_down: float32 [3072, 768], P('tensor', 'dp')
- d_gain_attn: float32 [768], replicated
- d_gain_mlp: float32 [768], replicated
- rms: float32 [3], replicated
Inputs may be any that keep to these rules, and one draw needn't show every extreme that they name: `pieces`: each aligned block of 256 tokens carries one number: 0 for text, or a positive number that no other block carries, for a picture piece. `lengths`: 2048 is reached in every draw.
All inputs are finite; a program needn't handle non-finite values.
Results may differ from a plain program's by a relative error of at most 0.018.
Values may be sent and summed in bfloat16 or wider, within the bound.
No kernel may reach another device: no remote copies, remote signals or barrier semaphores. Data moves between devices by JAX's collectives and lax.ppermute only.
A program may use at most 256 MiB of HBM per device.

v0:
```python
import math
import jax
import jax.numpy as jnp
from jax import lax
from jax.sharding import PartitionSpec as P

HD = 64
EPS = 1e-05
NEG = -1e30


def matmul(first_op, second_op):
    return jnp.dot(first_op, second_op, preferred_element_type=jnp.float32)


def matmul_tn(first_op, second_op):
    return lax.dot_general(
        first_op, second_op, (((0,), (0,)), ((), ())), preferred_element_type=jnp.float32
    )


def matmul_nt(first_op, second_op):
    return lax.dot_general(
        first_op, second_op, (((1,), (1,)), ((), ())), preferred_element_type=jnp.float32
    )


def norm_forward(resid, norm_gain):
    centred = resid - jnp.mean(resid, axis=-1, keepdims=True)
    inv_std = lax.rsqrt(jnp.mean(centred * centred, axis=-1, keepdims=True) + EPS)
    normed = centred * inv_std
    return (normed * norm_gain, normed, inv_std)


def norm_backward(upstream, norm_gain, normed, inv_std):
    scaled = upstream * norm_gain
    inner = (
        scaled
        - jnp.mean(scaled, axis=-1, keepdims=True)
        - normed * jnp.mean(scaled * normed, axis=-1, keepdims=True)
    )
    return (inner * inv_std, jnp.sum(upstream * normed, axis=0))


def visible_mask(pieces, valid_len, q_start, q_count, k_count):
    q_pos = q_start + lax.iota(jnp.int32, q_count)
    k_pos = lax.iota(jnp.int32, k_count)
    q_piece = pieces[q_start : q_start + q_count]
    k_piece = pieces[:k_count]
    same_piece = (q_piece[:, None] == k_piece[None, :]) & (q_piece[:, None] > 0)
    causal = k_pos[None, :] <= q_pos[:, None]
    return (k_pos[None, :] < valid_len) & (causal | same_piece)


def attend_forward(queries, key_rows, value_rows, pieces, valid_len):
    seq_len, head_cols = queries.shape
    local_heads = head_cols // HD
    scale_factor = 1.0 / math.sqrt(HD)
    block_rows = min(512, seq_len // 2)
    q_split = queries.reshape(seq_len, local_heads, HD)
    k_split = key_rows.reshape(seq_len, local_heads, HD)
    v_split = value_rows.reshape(seq_len, local_heads, HD)
    outputs = []
    log_sums = []
    for block_idx in range(seq_len // block_rows):
        q_start = block_idx * block_rows
        q_stop = q_start + block_rows
        raw_scores = (
            jnp.einsum(
                "qhd,khd->hqk",
                q_split[q_start:q_stop],
                k_split[:q_stop],
                preferred_element_type=jnp.float32,
            )
            * scale_factor
        )
        scores = jnp.where(
            visible_mask(pieces, valid_len, q_start, block_rows, q_stop)[None], raw_scores, NEG
        )
        row_max = jnp.max(scores, axis=-1, keepdims=True)
        exp_scores = jnp.exp(scores - row_max)
        row_total = jnp.sum(exp_scores, axis=-1, keepdims=True)
        attn_probs = (exp_scores / row_total).astype(jnp.bfloat16)
        head_out = jnp.einsum(
            "hqk,khd->qhd", attn_probs, v_split[:q_stop], preferred_element_type=jnp.float32
        )
        outputs.append(head_out.reshape(block_rows, head_cols).astype(jnp.bfloat16))
        log_sums.append(row_max + jnp.log(row_total))
    return (jnp.concatenate(outputs, axis=0), log_sums)


def attend_backward(queries, key_rows, value_rows, grad_heads, log_sums, pieces, valid_len):
    seq_len, head_cols = queries.shape
    local_heads = head_cols // HD
    scale_factor = 1.0 / math.sqrt(HD)
    block_rows = min(512, seq_len // 2)
    q_split = queries.reshape(seq_len, local_heads, HD)
    k_split = key_rows.reshape(seq_len, local_heads, HD)
    v_split = value_rows.reshape(seq_len, local_heads, HD)
    g_split = grad_heads.reshape(seq_len, local_heads, HD)
    grad_keys = jnp.zeros((seq_len, local_heads, HD), jnp.float32)
    grad_vals = jnp.zeros((seq_len, local_heads, HD), jnp.float32)
    grad_q_blocks = []
    for block_idx in range(seq_len // block_rows):
        q_start = block_idx * block_rows
        q_stop = q_start + block_rows
        q_block = q_split[q_start:q_stop]
        g_block = g_split[q_start:q_stop]
        raw_scores = (
            jnp.einsum(
                "qhd,khd->hqk", q_block, k_split[:q_stop], preferred_element_type=jnp.float32
            )
            * scale_factor
        )
        scores = jnp.where(
            visible_mask(pieces, valid_len, q_start, block_rows, q_stop)[None], raw_scores, NEG
        )
        attn_probs = jnp.exp(scores - log_sums[block_idx])
        low_probs = attn_probs.astype(jnp.bfloat16)
        grad_vals = grad_vals.at[:q_stop].add(
            jnp.einsum("hqk,qhd->khd", low_probs, g_block, preferred_element_type=jnp.float32)
        )
        grad_probs = jnp.einsum(
            "qhd,khd->hqk", g_block, v_split[:q_stop], preferred_element_type=jnp.float32
        )
        inner_sum = jnp.sum(attn_probs * grad_probs, axis=-1, keepdims=True)
        grad_scores = (attn_probs * (grad_probs - inner_sum)).astype(jnp.bfloat16)
        grad_q_blocks.append(
            jnp.einsum(
                "hqk,khd->qhd", grad_scores, k_split[:q_stop], preferred_element_type=jnp.float32
            )
            * scale_factor
        )
        grad_keys = grad_keys.at[:q_stop].add(
            jnp.einsum("hqk,qhd->khd", grad_scores, q_block, preferred_element_type=jnp.float32)
            * scale_factor
        )
    grad_q = jnp.concatenate(grad_q_blocks, axis=0).reshape(seq_len, head_cols)
    return (grad_q, grad_keys.reshape(seq_len, head_cols), grad_vals.reshape(seq_len, head_cols))


def gelu_tanh(pre_act):
    return jax.nn.gelu(pre_act, approximate=True)


def body(
    tokens,
    first_values,
    pieces,
    lengths,
    w_query,
    w_key,
    w_value,
    w_out,
    w_up,
    w_down,
    gain_attn,
    gain_mlp,
    cotangent,
):
    tensor_size = lax.axis_size("tensor")
    tensor_rank = lax.axis_index("tensor")
    fresh_ranks = tensor_size // 2
    local_rows, model_dim = tokens.shape
    seq_len = local_rows * tensor_size
    head_cols = w_query.shape[1]
    value_width = w_value.shape[1]
    valid_len = lengths[0]
    positions = tensor_rank * local_rows + lax.iota(jnp.int32, local_rows)
    valid = (positions < valid_len).astype(jnp.float32)[:, None]
    query_w, key_w, value_w, out_w, up_w, down_w = (
        lax.all_gather(w_query, "dp", axis=0, tiled=True),
        lax.all_gather(w_key, "dp", axis=0, tiled=True),
        lax.all_gather(w_value, "dp", axis=0, tiled=True),
        lax.all_gather(w_out, "dp", axis=1, tiled=True),
        lax.all_gather(w_up, "dp", axis=0, tiled=True),
        lax.all_gather(w_down, "dp", axis=1, tiled=True),
    )
    tokens_wide = tokens.astype(jnp.float32)
    norm_one, normed_one, inv_one = norm_forward(tokens_wide, gain_attn)
    attn_input = norm_one.astype(jnp.bfloat16)
    input_rows, first_rows = (
        lax.all_gather(attn_input, "tensor", axis=0, tiled=True),
        lax.all_gather(first_values, "tensor", axis=0, tiled=True),
    )
    queries = matmul(input_rows, query_w).astype(jnp.bfloat16)
    key_rows = matmul(input_rows, key_w).astype(jnp.bfloat16)

    def fresh_values(rows_in):
        value_cols = lax.dynamic_slice_in_dim(value_w, tensor_rank * head_cols, head_cols, 1)
        return matmul(rows_in, value_cols).astype(jnp.bfloat16)

    def reused_values(rows_in):
        return lax.dynamic_slice_in_dim(
            first_rows, (tensor_rank - fresh_ranks) * head_cols, head_cols, 1
        )

    value_rows = lax.cond(tensor_rank < fresh_ranks, fresh_values, reused_values, input_rows)
    heads_out, log_sums = attend_forward(queries, key_rows, value_rows, pieces, valid_len)
    attn_out = lax.psum_scatter(
        matmul(heads_out, out_w).astype(jnp.bfloat16), "tensor", scatter_dimension=0, tiled=True
    ).astype(jnp.float32)
    resid_mid = tokens_wide + attn_out
    norm_two, normed_two, inv_two = norm_forward(resid_mid, gain_mlp)
    mlp_input = norm_two.astype(jnp.bfloat16)
    mlp_rows = lax.all_gather(mlp_input, "tensor", axis=0, tiled=True)
    up_pre = matmul(mlp_rows, up_w)
    hidden_act, gelu_pull = jax.vjp(gelu_tanh, up_pre)
    hidden = hidden_act.astype(jnp.bfloat16)
    mlp_out = lax.psum_scatter(
        matmul(hidden, down_w).astype(jnp.bfloat16), "tensor", scatter_dimension=0, tiled=True
    ).astype(jnp.float32)
    final = resid_mid + mlp_out
    squares = jnp.stack(
        [
            jnp.sum(valid * final * final),
            jnp.sum(valid * attn_out * attn_out),
            jnp.sum(valid * mlp_out * mlp_out),
            jnp.sum(valid),
        ]
    )
    query_w, key_w, value_w, out_w, up_w, down_w = (
        lax.all_gather(w_query, "dp", axis=0, tiled=True),
        lax.all_gather(w_key, "dp", axis=0, tiled=True),
        lax.all_gather(w_value, "dp", axis=0, tiled=True),
        lax.all_gather(w_out, "dp", axis=1, tiled=True),
        lax.all_gather(w_up, "dp", axis=0, tiled=True),
        lax.all_gather(w_down, "dp", axis=1, tiled=True),
    )
    out_grad = cotangent.astype(jnp.float32)
    cot_rows = lax.all_gather(cotangent, "tensor", axis=0, tiled=True)
    grad_down_w = matmul_tn(hidden, cot_rows)
    grad_hidden = matmul_nt(cot_rows, down_w)
    grad_up_pre = gelu_pull(grad_hidden)[0].astype(jnp.bfloat16)
    grad_up_w = matmul_tn(mlp_rows, grad_up_pre)
    grad_mlp_input = lax.psum_scatter(
        matmul_nt(grad_up_pre, up_w).astype(jnp.bfloat16), "tensor", scatter_dimension=0, tiled=True
    ).astype(jnp.float32)
    grad_two, gain_two_grad = norm_backward(grad_mlp_input, gain_mlp, normed_two, inv_two)
    resid_grad = out_grad + grad_two
    resid_rows = lax.all_gather(resid_grad.astype(jnp.bfloat16), "tensor", axis=0, tiled=True)
    grad_out_w = matmul_tn(heads_out, resid_rows)
    grad_heads = matmul_nt(resid_rows, out_w).astype(jnp.bfloat16)
    grad_q, grad_k, grad_v = attend_backward(
        queries, key_rows, value_rows, grad_heads, log_sums, pieces, valid_len
    )
    grad_q_low = grad_q.astype(jnp.bfloat16)
    grad_k_low = grad_k.astype(jnp.bfloat16)
    grad_query_w = matmul_tn(input_rows, grad_q_low)
    grad_key_w = matmul_tn(input_rows, grad_k_low)
    input_part = matmul_nt(grad_q_low, query_w) + matmul_nt(grad_k_low, key_w)

    def fresh_back(grad_vals):
        grad_low = grad_vals.astype(jnp.bfloat16)
        value_cols = lax.dynamic_slice_in_dim(value_w, tensor_rank * head_cols, head_cols, 1)
        grad_cols = matmul_tn(input_rows, grad_low)
        grad_value_full = lax.dynamic_update_slice_in_dim(
            jnp.zeros((model_dim, value_width), jnp.float32), grad_cols, tensor_rank * head_cols, 1
        )
        return (
            grad_value_full,
            matmul_nt(grad_low, value_cols),
            jnp.zeros((seq_len, value_width), jnp.float32),
        )

    def reused_back(grad_vals):
        first_part = lax.dynamic_update_slice_in_dim(
            jnp.zeros((seq_len, value_width), jnp.float32),
            grad_vals,
            (tensor_rank - fresh_ranks) * head_cols,
            1,
        )
        return (
            jnp.zeros((model_dim, value_width), jnp.float32),
            jnp.zeros((seq_len, model_dim), jnp.float32),
            first_part,
        )

    grad_value_w, value_input, first_part = lax.cond(
        tensor_rank < fresh_ranks, fresh_back, reused_back, grad_v
    )
    grad_attn_input, first_grad = (
        lax.psum_scatter(
            (input_part + value_input).astype(jnp.bfloat16),
            "tensor",
            scatter_dimension=0,
            tiled=True,
        ).astype(jnp.float32),
        lax.psum_scatter(
            first_part.astype(jnp.bfloat16), "tensor", scatter_dimension=0, tiled=True
        ).astype(jnp.float32),
    )
    grad_one, gain_one_grad = norm_backward(grad_attn_input, gain_attn, normed_one, inv_one)
    token_grad = resid_grad + grad_one
    grad_query_w, grad_key_w, grad_out_w, grad_up_w, grad_down_w = (
        lax.psum_scatter(grad_query_w, "dp", scatter_dimension=0, tiled=True),
        lax.psum_scatter(grad_key_w, "dp", scatter_dimension=0, tiled=True),
        lax.psum_scatter(grad_out_w, "dp", scatter_dimension=1, tiled=True),
        lax.psum_scatter(grad_up_w, "dp", scatter_dimension=0, tiled=True),
        lax.psum_scatter(grad_down_w, "dp", scatter_dimension=1, tiled=True),
    )
    value_total, gain_one_total, gain_two_total, square_total = lax.psum(
        (grad_value_w, gain_one_grad, gain_two_grad, squares), ("dp", "tensor")
    )
    share_rows = value_total.shape[0] // lax.axis_size("dp")
    value_share = lax.dynamic_slice_in_dim(
        value_total, lax.axis_index("dp") * share_rows, share_rows, 0
    )
    rms = jnp.sqrt(square_total[:3] / (square_total[3] * model_dim))
    return (
        final.astype(jnp.bfloat16),
        token_grad,
        first_grad,
        grad_query_w,
        grad_key_w,
        value_share,
        grad_out_w,
        grad_up_w,
        grad_down_w,
        gain_one_total,
        gain_two_total,
        rms,
    )


def solution(mesh):
    in_specs = (
        P(("dp", "tensor"), None),
        P(("dp", "tensor"), None),
        P("dp"),
        P("dp"),
        P("dp", "tensor"),
        P("dp", "tensor"),
        P("dp", None),
        P("tensor", "dp"),
        P("dp", "tensor"),
        P("tensor", "dp"),
        P(),
        P(),
        P(("dp", "tensor"), None),
    )
    out_specs = (
        P(("dp", "tensor"), None),
        P(("dp", "tensor"), None),
        P(("dp", "tensor"), None),
        P("dp", "tensor"),
        P("dp", "tensor"),
        P("dp", None),
        P("tensor", "dp"),
        P("dp", "tensor"),
        P("tensor", "dp"),
        P(),
        P(),
        P(),
    )
    return jax.shard_map(body, mesh=mesh, in_specs=in_specs, out_specs=out_specs, check_vma=False)
```

profile of v0, /device:TPU:0, one launch (start us, length us, event | category | flops | bytes accessed | tf_op | source)
XLA Modules:
  0.0 1069.0 jit_solution(11694905929463329441)
XLA Ops:
  16.4 35.0 %all_gather.44 = bf16[192,768]{0,1:T(8,128)(2,1)} all-gather(bf16[192,96]{0,1:T(8,128)(2,1)S(1)} %copy.36), channel_id=1, replica_groups=mesh['dp'=8,'tensor'=4] {'dp'}, dimensions={1}, use_global_device_ids=true | all-gather | bytes 331776 | tf_op jit(solution)/shard_map/all_gather | solution.py:175
  51.4 31.3 %all_gather.42 = bf16[768,192]{1,0:T(8,128)(2,1)S(1)} all-gather(bf16[96,192]{1,0:T(8,128)(2,1)S(1)} %copy-done.70), channel_id=1, replica_groups=mesh['dp'=8,'tensor'=4] {'dp'}, dimensions={0}, use_global_device_ids=true | all-gather | bytes 331776 | tf_op jit(solution)/shard_map/all_gather | solution.py:172
  82.6 31.0 %all_gather.43 = bf16[768,192]{1,0:T(8,128)(2,1)S(1)} all-gather(bf16[96,192]{1,0:T(8,128)(2,1)S(1)} %copy-done.71), channel_id=1, replica_groups=mesh['dp'=8,'tensor'=4] {'dp'}, dimensions={0}, use_global_device_ids=true | all-gather | bytes 331776 | tf_op jit(solution)/shard_map/all_gather | solution.py:173
  116.2 33.7 %all_gather.40 = bf16[768,384]{1,0:T(8,128)(2,1)} all-gather(bf16[96,384]{1,0:T(8,128)(2,1)S(1)} %copy-done.63), channel_id=1, replica_groups=mesh['dp'=8,'tensor'=4] {'dp'}, dimensions={0}, use_global_device_ids=true | all-gather | bytes 663552 | tf_op jit(solution)/shard_map/all_gather | solution.py:174
  149.9 2.4 fusion.29
  153.6 3.8 conditional.2
  153.6 3.5 fusion
  157.6 3.7 convolution_convert_fusion.5
  170.2 2.2 fusion.113
  172.4 2.0 fusion.132
  175.9 2.2 copy-done.1
  178.2 2.3 fusion.107
  180.5 2.7 fusion.131
  185.1 2.7 copy-done
  187.8 3.1 fusion.114
  191.6 2.7 convolution_convert_fusion.3
  196.3 36.2 %reduce-scatter.13.cloned.1.call-done = bf16[512,768]{1,0:T(8,128)(2,1)} async-done(((bf16[2048,768]{1,0:T(8,128)(2,1)}), bf16[512,768]{1,0:T(8,128)(2,1)}) %reduce-scatter.13.cloned.1.call-update) | async-done | bytes 786448 | tf_op jit(solution)/shard_map/reduce_scatter | solution.py:200
  238.8 28.4 %all-gather.18.cloned.1.call-done = bf16[2048,768]{1,0:T(8,128)(2,1)} async-done(((bf16[512,768]{1,0:T(8,128)(2,1)}), bf16[2048,768]{1,0:T(8,128)(2,1)}) %all-gather.18.cloned.1.call-update) | async-done | bytes 3145744 | tf_op jit(solution)/shard_map/all_gather | solution.py:231
  267.2 7.4 fusion.135
  274.6 36.4 %all-gather.14.cloned.1.call-done = bf16[768,768]{1,0:T(8,128)(2,1)} async-done(((bf16[96,768]{1,0:T(8,128)(2,1)}), bf16[768,768]{1,0:T(8,128)(2,1)}) %all-gather.14.cloned.1.call-update) | async-done | bytes 1179664 | tf_op jit(solution)/shard_map/all_gather | solution.py:176
  311.1 29.1 %all-gather.12.cloned.1.call-done = bf16[2048,768]{1,0:T(8,128)(2,1)} async-done(((bf16[512,768]{1,0:T(8,128)(2,1)}), bf16[2048,768]{1,0:T(8,128)(2,1)}) %all-gather.12.cloned.1.call-update) | async-done | bytes 3145744 | tf_op jit(solution)/shard_map/all_gather | solution.py:206
  340.2 10.0 fusion.17
  351.8 4.1 convolution_convert_fusion.1
  357.2 8.3 convolution_convert_fusion.2
  365.8 28.3 %reduce-scatter.17.cloned.1.call-done = bf16[512,768]{1,0:T(8,128)(2,1)} async-done(((bf16[2048,768]{1,0:T(8,128)(2,1)}), bf16[512,768]{1,0:T(8,128)(2,1)}) %reduce-scatter.17.cloned.1.call-update) | async-done | bytes 786448 | tf_op jit(solution)/shard_map/reduce_scatter | solution.py:236
  394.1 40.4 %reduce-scatter.15.cloned.1.call-done = bf16[512,768]{1,0:T(8,128)(2,1)} async-done(((bf16[2048,768]{1,0:T(8,128)(2,1)}), bf16[512,768]{1,0:T(8,128)(2,1)}) %reduce-scatter.15.cloned.1.call-update) | async-done | bytes 786448 | tf_op jit(solution)/shard_map/reduce_scatter | solution.py:210
  434.5 4.5 fusion.80
  439.0 3.1 fusion.126
  442.3 28.3 %all-gather.20.cloned.1.call-done = bf16[2048,768]{1,0:T(8,128)(2,1)} async-done(((bf16[512,768]{1,0:T(8,128)(2,1)}), bf16[2048,768]{1,0:T(8,128)(2,1)}) %all-gather.20.cloned.1.call-update) | async-done | bytes 3145744 | tf_op jit(solution)/shard_map/all_gather | solution.py:241
  470.7 3.3 convolution_convert_fusion.4
  474.9 3.0 multiply_reduce_fusion.3
  478.1 8.9 multiply_reduce_fusion.1
  488.3 2.1 fusion.51
  491.4 2.2 fusion.54
  493.5 17.0 %conditional.3 = (f32[768,384]{0,1:T(8,128)}, bf16[2048,384]{1,0:T(8,128)(2,1)S(1)}, f32[2048,768]{1,0:T(8,128)}) conditional(s32[]{:T(128)} %convert_element_type.169, (s32[]{:T(128)}, bf16[2048,192]{0,1:T(8,128)(2,1)S(1)}) %tuple.159, (bf16[2048,192]{0,1:T(8,128)(2,1)S(1)}, bf16[2048,768]{1,0:T(8,128)(2,1)}, s32[]{:T(128)}, ...), branch_computations={%region_23.24_spmd, %region_24.25_spmd} | conditional | flops 1207959552 | bytes 28901462 | solution.py:279
  495.6 3.5 convolution_dynamic-update-slice_fusion
  499.1 4.8 convolution_bitcast_fusion
  503.9 6.6 copy.51
  510.6 3.3 copy.43
  514.0 7.4 multiply_convert_fusion.1
  521.4 2.2 copy-done.6
  523.7 2.2 fusion.118
  525.9 2.2 convolution_bitcast_fusion.1
  528.2 5.5 multiply_reduce_fusion.2
  533.8 3.9 multiply_convert_fusion.4
  538.5 3.8 multiply_convert_fusion.2
  546.4 6.5 multiply_reduce_fusion
  553.2 9.5 multiply_convert_fusion
  571.5 5.7 add_convert_fusion
  577.3 7.0 fusion.139
  584.6 8.3 fusion.127
  593.0 3.8 fusion.138
  597.5 2.5 pad_maximum_fusion.4
  600.0 3.8 fusion.137
  603.9 43.7 %all-reduce.5.cloned.1.call-done = f32[768,384]{1,0:T(8,128)} async-done(((f32[768,384]{1,0:T(8,128)}), f32[768,384]{1,0:T(8,128)}) %all-reduce.5.cloned.1.call-update) | async-done | bytes 1179664 | tf_op jit(solution)/shard_map/psum | solution.py:302
  649.2 63.5 %reduce-scatter.31.cloned.1.call-done = f32[96,192]{1,0:T(8,128)} async-done(((f32[768,192]{1,0:T(8,128)}), f32[96,192]{1,0:T(8,128)}) %reduce-scatter.31.cloned.1.call-update) | async-done | bytes 73744
  714.3 28.7 %reduce-scatter.21.cloned.1.call-done = bf16[512,384]{1,0:T(8,128)(2,1)} async-done(((bf16[2048,384]{1,0:T(8,128)(2,1)}), bf16[512,384]{1,0:T(8,128)(2,1)}) %reduce-scatter.21.cloned.1.call-update) | async-done | bytes 393232 | tf_op jit(solution)/shard_map/reduce_scatter | solution.py:289
  744.9 38.3 %reduce-scatter.19.cloned.1.call-done = bf16[512,768]{1,0:T(8,128)(2,1)} async-done(((bf16[2048,768]{1,0:T(8,128)(2,1)}), bf16[512,768]{1,0:T(8,128)(2,1)}) %reduce-scatter.19.cloned.1.call-update) | async-done | bytes 786448 | tf_op jit(solution)/shard_map/reduce_scatter | solution.py:283
  785.2 41.1 %all-reduce.2 = (f32[768]{0:T(1024)}, f32[768]{0:T(1024)}, f32[4]{0:T(128)S(1)}) all-reduce(f32[768]{0:T(1024)S(1)} %get-tuple-element.223, f32[768]{0:T(1024)S(1)} %copy-done.86, f32[4]{0:T(128)S(1)} %pad_maximum_fusion.4), channel_id=1, replica_groups=mesh['dp'=8,'tensor'=4] {'dp','tensor'}, use_global_device_ids=true, to_apply=%region_36.37 | all-reduce | flops 1540 | bytes 12320 | tf_op jit(solution)/shard_map/psum | solution.py:302
  828.1 3.2 fusion.74
  831.4 26.2 %reduce-scatter.27.cloned.1.call-done = f32[96,768]{1,0:T(8,128)} async-done(((f32[768,768]{1,0:T(8,128)}), f32[96,768]{1,0:T(8,128)}) %reduce-scatter.27.cloned.1.call-update) | async-done | bytes 294928 | tf_op jit(solution)/shard_map/reduce_scatter | solution.py:299
  857.5 72.6 %reduce-scatter.29.cloned.1.call-done = f32[768,96]{0,1:T(8,128)} async-done(((f32[768,768]{0,1:T(8,128)}), f32[768,96]{0,1:T(8,128)}) %reduce-scatter.29.cloned.1.call-update) | async-done | bytes 294928 | tf_op jit(solution)/shard_map/reduce_scatter | solution.py:300
  930.1 65.9 %reduce-scatter.25.cloned.1.call-done = f32[96,192]{1,0:T(8,128)} async-done(((f32[768,192]{1,0:T(8,128)}), f32[96,192]{1,0:T(8,128)}) %reduce-scatter.25.cloned.1.call-update) | async-done | bytes 73744 | tf_op jit(solution)/shard_map/reduce_scatter | solution.py:297
  996.1 65.4 %reduce-scatter.23.cloned.1.call-done = f32[96,192]{1,0:T(8,128)} async-done(((f32[768,192]{1,0:T(8,128)}), f32[96,192]{1,0:T(8,128)}) %reduce-scatter.23.cloned.1.call-update) | async-done | bytes 73744 | tf_op jit(solution)/shard_map/reduce_scatter | solution.py:296
  (336 shorter events, 64.2 us)
Async XLA Ops:
  8.0 43.3 %copy-start.70 = (bf16[96,192]{1,0:T(8,128)(2,1)S(1)}, bf16[96,192]{1,0:T(8,128)(2,1)}, u32[]{:S(2)}) copy-start(bf16[96,192]{1,0:T(8,128)(2,1)} %param.41) | copy-start | bytes 110596
  8.0 74.6 %copy-start.71 = (bf16[96,192]{1,0:T(8,128)(2,1)S(1)}, bf16[96,192]{1,0:T(8,128)(2,1)}, u32[]{:S(2)}) copy-start(bf16[96,192]{1,0:T(8,128)(2,1)} %param.42) | copy-start | bytes 110596
  8.1 105.6 %copy-start.54 = (s32[2048]{0:T(1024)S(1)}, s32[2048]{0:T(1024)}, u32[]{:S(2)}) copy-start(s32[2048]{0:T(1024)} %param.39) | copy-start | bytes 24580
  8.1 145.5 %all-gather.8.cloned.1.call-start = ((), (), s32[]{:S(2)}) async-start(), calls=%async_computation.10 | async-start | bytes 1966080 | tf_op jit(solution)/shard_map/all_gather | solution.py:184
  10.1 104.6 %slice-start.13 = ((s32[2048]{0:T(1024)}), s32[1024]{0:T(1024)S(1)}, s32[]{:S(2)}) async-start(s32[2048]{0:T(1024)} %param.39), calls=%async_computation.41 | async-start | bytes 8192 | tf_op jit(solution)/shard_map/slice | solution.py:49
  10.1 106.0 %copy-start.63 = (bf16[96,384]{1,0:T(8,128)(2,1)S(1)}, bf16[96,384]{1,0:T(8,128)(2,1)}, u32[]{:S(2)}) copy-start(bf16[96,384]{1,0:T(8,128)(2,1)} %param.43) | copy-start | bytes 221188
  10.1 143.4 %all-gather.10.cloned.1.call-start = ((), (), s32[]{:S(2)}) async-start(), calls=%async_computation.11 | async-start | bytes 3932160 | tf_op jit(solution)/shard_map/all_gather | solution.py:183
  15.5 217.0 %reduce-scatter.13.cloned.1.call-start = ((), (), s32[]{:S(2)}) async-start(), calls=%async_computation.12 | async-start | bytes 3932160 | tf_op jit(solution)/shard_map/reduce_scatter | solution.py:200
  82.6 78.7 %copy-start.23 = (bf16[768,192]{1,0:T(8,128)(2,1)}, bf16[768,192]{1,0:T(8,128)(2,1)S(1)}, u32[]{:S(2)}) copy-start(bf16[768,192]{1,0:T(8,128)(2,1)S(1)} %all_gather.42) | copy-start | bytes 884740
  113.6 43.9 %copy-start.25 = (bf16[768,192]{1,0:T(8,128)(2,1)}, bf16[768,192]{1,0:T(8,128)(2,1)S(1)}, u32[]{:S(2)}) copy-start(bf16[768,192]{1,0:T(8,128)(2,1)S(1)} %all_gather.43) | copy-start | bytes 884740
  157.4 27.7 %copy-start.13 = (bf16[2048,192]{0,1:T(8,128)(2,1)}, bf16[2048,192]{0,1:T(8,128)(2,1)S(1)}, u32[]{:S(2)}) copy-start(bf16[2048,192]{0,1:T(8,128)(2,1)S(1)} %get-tuple-element.276) | copy-start | bytes 2359300
  157.5 11.5 %copy-start.43 = (bf16[1024,192]{0,1:T(8,128)(2,1)}, bf16[1024,192]{0,1:T(8,128)(2,1)S(1)}, u32[]{:S(2)}) copy-start(bf16[1024,192]{0,1:T(8,128)(2,1)S(1)} %slice.378) | copy-start | bytes 1179652
  157.6 18.3 %copy-start.28 = (bf16[1536,192]{0,1:T(8,128)(2,1)}, bf16[1536,192]{0,1:T(8,128)(2,1)S(1)}, u32[]{:S(2)}) copy-start(bf16[1536,192]{0,1:T(8,128)(2,1)S(1)} %slice.381) | copy-start | bytes 1769476
  161.2 19.3 %copy-start.15 = (bf16[2048,192]{0,1:T(8,128)(2,1)}, bf16[2048,192]{0,1:T(8,128)(2,1)S(1)}, u32[]{:S(2)}) copy-start(bf16[2048,192]{0,1:T(8,128)(2,1)S(1)} %convolution_convert_fusion.5) | copy-start | bytes 2359300
  161.4 11.0 %copy-start.21 = (bf16[1536,192]{0,1:T(8,128)(2,1)}, bf16[1536,192]{0,1:T(8,128)(2,1)S(1)}, u32[]{:S(2)}) copy-start(bf16[1536,192]{0,1:T(8,128)(2,1)S(1)} %slice.383) | copy-start | bytes 1769476
  172.4 18.5 %copy-start.91 = (bf16[3,64,512]{2,1,0:T(8,128)(2,1)}, bf16[3,64,512]{2,1,0:T(8,128)(2,1)S(1)}, u32[]{:S(2)}) copy-start(bf16[3,64,512]{2,1,0:T(8,128)(2,1)S(1)} %fusion.113) | copy-start | bytes 589828
  180.5 10.4 copy-start.93
  194.3 41.3 %copy-start.64 = (f32[768]{0:T(1024)S(1)}, f32[768]{0:T(1024)}, u32[]{:S(2)}) copy-start(f32[768]{0:T(1024)} %param.48) | copy-start | bytes 9220
  194.3 44.5 %all-gather.16.cloned.1.call-start = ((), (), s32[]{:S(2)}) async-start(), calls=%async_computation.15 | async-start | bytes 1327104 | tf_op jit(solution)/shard_map/all_gather | solution.py:177
  194.9 72.3 %all-gather.18.cloned.1.call-start = ((), (), s32[]{:S(2)}) async-start(), calls=%async_computation.17 | async-start | bytes 3932160 | tf_op jit(solution)/shard_map/all_gather | solution.py:231
  195.5 115.6 %all-gather.14.cloned.1.call-start = ((), (), s32[]{:S(2)}) async-start(), calls=%async_computation.14 | async-start | bytes 1327104 | tf_op jit(solution)/shard_map/all_gather | solution.py:176
  196.1 144.1 %all-gather.12.cloned.1.call-start = ((), (), s32[]{:S(2)}) async-start(), calls=%async_computation.13 | async-start | bytes 3932160 | tf_op jit(solution)/shard_map/all_gather | solution.py:206
  234.0 205.0 %copy-start.59 = (f32[512]{0:T(512)}, f32[512]{0:T(512)S(1)}, u32[]{:S(2)}) copy-start(f32[512]{0:T(512)S(1)} %broadcast_multiply_fusion.4) | copy-start | bytes 6148
  235.6 203.4 %copy-start.68 = (f32[512]{0:T(512)}, f32[512]{0:T(512)S(1)}, u32[]{:S(2)}) copy-start(f32[512]{0:T(512)S(1)} %add_rsqrt_fusion) | copy-start | bytes 6148
  236.8 157.2 %reduce-scatter.17.cloned.1.call-start = ((), (), s32[]{:S(2)}) async-start(), calls=%async_computation.18 | async-start | bytes 3932160 | tf_op jit(solution)/shard_map/reduce_scatter | solution.py:236
  311.1 40.8 %copy-start.88 = (bf16[768,768]{1,0:T(8,128)(2,1)S(1)}, bf16[768,768]{1,0:T(8,128)(2,1)}, u32[]{:S(2)}) copy-start(bf16[768,768]{1,0:T(8,128)(2,1)} %all-gather.14.cloned.1.call-done) | copy-start | bytes 3538948
  356.0 78.5 %reduce-scatter.15.cloned.1.call-start = ((), (), s32[]{:S(2)}) async-start(), calls=%async_computation.16 | async-start | bytes 3932160 | tf_op jit(solution)/shard_map/reduce_scatter | solution.py:210
  365.5 105.1 %all-gather.20.cloned.1.call-start = ((), (), s32[]{:S(2)}) async-start(), calls=%async_computation.19 | async-start | bytes 3932160 | tf_op jit(solution)/shard_map/all_gather | solution.py:241
  438.9 31.7 %copy-start.82 = (f32[512]{0:T(512)}, f32[512]{0:T(512)S(1)}, u32[]{:S(2)}) copy-start(f32[512]{0:T(512)S(1)} %get-tuple-element.268) | copy-start | bytes 6148
  438.9 31.7 %copy-start.84 = (f32[512]{0:T(512)}, f32[512]{0:T(512)S(1)}, u32[]{:S(2)}) copy-start(f32[512]{0:T(512)S(1)} %get-tuple-element.269) | copy-start | bytes 6148
  439.0 48.0 %slice-start.9 = ((s8[6291456]{0:T(1024)(128)(4,1)}), s8[2097152]{0:T(1024)(128)(4,1)S(1)}, s32[]{:S(2)}) async-start(s8[6291456]{0:T(1024)(128)(4,1)} %bitcast.173), calls=%async_computation.37 | async-start | bytes 4194304
  442.2 205.4 %all-reduce.5.cloned.1.call-start = ((), (), s32[]{:S(2)}) async-start(), calls=%async_computation.24 | async-start | bytes 2359296 | tf_op jit(solution)/shard_map/psum | solution.py:302
  442.2 32.4 %copy-start.57 = (f32[3,512]{1,0:T(4,128)}, f32[3,512]{1,0:T(4,128)S(1)}, u32[]{:S(2)}) copy-start(f32[3,512]{1,0:T(4,128)S(1)} %log_add_fusion.3) | copy-start | bytes 18436
  442.3 44.7 %copy-start.55 = (f32[3,512]{1,0:T(4,128)}, f32[3,512]{1,0:T(4,128)S(1)}, u32[]{:S(2)}) copy-start(f32[3,512]{1,0:T(4,128)S(1)} %log_add_fusion.2) | copy-start | bytes 18436
  474.0 13.0 %copy-start.41 = (bf16[512,192]{0,1:T(8,128)(2,1)}, bf16[512,192]{0,1:T(8,128)(2,1)S(1)}, u32[]{:S(2)}) copy-start(bf16[512,192]{0,1:T(8,128)(2,1)S(1)} %get-tuple-element.236) | copy-start | bytes 589828
  474.0 16.4 %copy-start.30 = (bf16[512,192]{0,1:T(8,128)(2,1)}, bf16[512,192]{0,1:T(8,128)(2,1)S(1)}, u32[]{:S(2)}) copy-start(bf16[512,192]{0,1:T(8,128)(2,1)S(1)} %get-tuple-element.234) | copy-start | bytes 589828
  474.9 13.4 %slice-start.6 = ((s8[9437184]{0:T(1024)(128)(4,1)}), s8[4194304]{0:T(1024)(128)(4,1)S(1)}, s32[]{:S(2)}) async-start(s8[9437184]{0:T(1024)(128)(4,1)} %bitcast.171), calls=%async_computation.34 | async-start | bytes 8388608
  478.1 10.2 slice-start.7
  478.1 10.2 slice-start.8
  478.1 12.3 %slice-start = ((s8[12582912]{0:T(1024)(128)(4,1)}), s8[4194304]{0:T(1024)(128)(4,1)S(1)}, s32[]{:S(2)}) async-start(s8[12582912]{0:T(1024)(128)(4,1)} %bitcast.167), calls=%async_computation.28 | async-start | bytes 8388608
  478.1 12.3 %slice-start.1 = ((s8[12582912]{0:T(1024)(128)(4,1)}), s8[4194304]{0:T(1024)(128)(4,1)S(1)}, s32[]{:S(2)}) async-start(s8[12582912]{0:T(1024)(128)(4,1)} %bitcast.167), calls=%async_computation.29 | async-start | bytes 8388608
  510.6 10.9 %copy-start.20 = (bf16[2048,384]{1,0:T(8,128)(2,1)}, bf16[2048,384]{1,0:T(8,128)(2,1)S(1)}, u32[]{:S(2)}) copy-start(bf16[2048,384]{1,0:T(8,128)(2,1)S(1)} %get-tuple-element.206) | copy-start | bytes 4718596
  513.9 198.8 %reduce-scatter.31.cloned.1.call-start = ((), (), s32[]{:S(2)}) async-start(), calls=%async_computation.27 | async-start | bytes 884736
  514.0 9.7 copy-start.22
  533.7 209.3 %reduce-scatter.21.cloned.1.call-start = ((), (), s32[]{:S(2)}) async-start(), calls=%async_computation.21 | async-start | bytes 1966080 | tf_op jit(solution)/shard_map/reduce_scatter | solution.py:289
  533.8 12.6 %slice-start.3 = ((s8[12582912]{0:T(1024)(128)(4,1)}), s8[4194304]{0:T(1024)(128)(4,1)S(1)}, s32[]{:S(2)}) async-start(s8[12582912]{0:T(1024)(128)(4,1)} %bitcast.169), calls=%async_computation.31 | async-start | bytes 8388608
  552.9 230.3 %reduce-scatter.19.cloned.1.call-start = ((), (), s32[]{:S(2)}) async-start(), calls=%async_computation.20 | async-start | bytes 3932160 | tf_op jit(solution)/shard_map/reduce_scatter | solution.py:283
  553.2 9.5 copy-start.40
  577.3 280.3 %reduce-scatter.27.cloned.1.call-start = ((), (), s32[]{:S(2)}) async-start(), calls=%async_computation.25 | async-start | bytes 2654208 | tf_op jit(solution)/shard_map/reduce_scatter | solution.py:299
  584.3 345.8 %reduce-scatter.29.cloned.1.call-start = ((), (), s32[]{:S(2)}) async-start(), calls=%async_computation.26 | async-start | bytes 2654208 | tf_op jit(solution)/shard_map/reduce_scatter | solution.py:300
  592.9 403.1 %reduce-scatter.25.cloned.1.call-start = ((), (), s32[]{:S(2)}) async-start(), calls=%async_computation.23 | async-start | bytes 884736 | tf_op jit(solution)/shard_map/reduce_scatter | solution.py:297
  596.8 464.6 %reduce-scatter.23.cloned.1.call-start = ((), (), s32[]{:S(2)}) async-start(), calls=%async_computation.22 | async-start | bytes 884736 | tf_op jit(solution)/shard_map/reduce_scatter | solution.py:296
  600.0 183.3 %copy-start.67 = (f32[512]{0:T(512)S(1)}, f32[512]{0:T(512)}, u32[]{:S(2)}) copy-start(f32[512]{0:T(512)} %copy-done.66) | copy-start | bytes 6148
  600.0 183.3 %copy-start.73 = (f32[768]{0:T(1024)S(1)}, f32[768]{0:T(1024)}, u32[]{:S(2)}) copy-start(f32[768]{0:T(1024)} %param.47) | copy-start | bytes 9220
  600.0 183.3 %copy-start.76 = (f32[512]{0:T(512)S(1)}, f32[512]{0:T(512)}, u32[]{:S(2)}) copy-start(f32[512]{0:T(512)} %copy-done.75) | copy-start | bytes 6148
  603.8 181.4 %copy-start.86 = (f32[768]{0:T(1024)S(1)}, f32[768]{0:T(1024)}, u32[]{:S(2)}) copy-start(f32[768]{0:T(1024)} %get-tuple-element.221) | copy-start | bytes 9220
  603.8 224.3 %copy-start.11 = (bf16[512,768]{1,0:T(8,128)(2,1)S(1)}, bf16[512,768]{1,0:T(8,128)(2,1)}, u32[]{:S(2)}) copy-start(bf16[512,768]{1,0:T(8,128)(2,1)} %reduce-scatter.13.cloned.1.call-done) | copy-start | bytes 2359300
  603.8 224.3 %copy-start.17 = (bf16[512,768]{1,0:T(8,128)(2,1)S(1)}, bf16[512,768]{1,0:T(8,128)(2,1)}, u32[]{:S(2)}) copy-start(bf16[512,768]{1,0:T(8,128)(2,1)} %param.49) | copy-start | bytes 2359300
  603.8 224.3 %copy-start.19 = (bf16[512,768]{1,0:T(8,128)(2,1)S(1)}, bf16[512,768]{1,0:T(8,128)(2,1)}, u32[]{:S(2)}) copy-start(bf16[512,768]{1,0:T(8,128)(2,1)} %reduce-scatter.17.cloned.1.call-done) | copy-start | bytes 2359300
  603.8 224.3 %copy-start.60 = (f32[512]{0:T(512)S(1)}, f32[512]{0:T(512)}, u32[]{:S(2)}) copy-start(f32[512]{0:T(512)} %copy-done.59) | copy-start | bytes 6148
  603.8 224.3 %copy-start.65 = (f32[768]{0:T(1024)S(1)}, f32[768]{0:T(1024)}, u32[]{:S(2)}) copy-start(f32[768]{0:T(1024)} %param.48) | copy-start | bytes 9220
  603.8 224.3 %copy-start.69 = (f32[512]{0:T(512)S(1)}, f32[512]{0:T(512)}, u32[]{:S(2)}) copy-start(f32[512]{0:T(512)} %copy-done.68) | copy-start | bytes 6148
  603.8 224.3 %copy-start.83 = (f32[512]{0:T(512)S(1)}, f32[512]{0:T(512)}, u32[]{:S(2)}) copy-start(f32[512]{0:T(512)} %copy-done.82) | copy-start | bytes 6148
  603.8 224.3 %copy-start.85 = (f32[512]{0:T(512)S(1)}, f32[512]{0:T(512)}, u32[]{:S(2)}) copy-start(f32[512]{0:T(512)} %copy-done.84) | copy-start | bytes 6148
  (66 other events, 204.8 us)
Sparse Core Ops, SparseCore 0:
  10.5 22.3 all-gather.7
  35.0 28.5 all-gather.9
  194.5 38.0 reduce-scatter.12
  356.1 37.9 reduce-scatter.16
  396.5 37.9 reduce-scatter.14
Sparse Core Ops, SparseCore 1:
  197.2 41.5 all-gather.15
  240.3 26.8 all-gather.17
  269.5 41.5 all-gather.13
  313.3 26.8 all-gather.11
  442.2 28.3 all-gather.19
  514.0 133.5 all-reduce.4
  651.3 61.3 reduce-scatter.30
  715.8 27.1 reduce-scatter.20
  745.4 37.8 reduce-scatter.18
  787.7 69.8 reduce-scatter.26
  861.9 68.2 reduce-scatter.28
  934.4 61.6 reduce-scatter.24
  999.8 61.6 reduce-scatter.22
where the time goes:
time: 1070 us
  waiting for transfers between devices  635 us (59%)
  blocking collectives  172 us (16%)
  matrix products  140 us (13%)
  other arithmetic  63.5 us (6%)
  local copies, waits for them, and re-layouts  37.3 us (3%)
  between operations  18.6 us (2%)
    reduce_scatter x1, waiting for transfers between devices, body(): lax.psum_scatter(grad_down_w, 'dp', scatter_dimension=1, tiled=True)  72.6 us
    reduce_scatter x1, waiting for transfers between devices, body(): lax.psum_scatter(grad_key_w, 'dp', scatter_dimension=0, tiled=True)  65.9 us
    reduce_scatter x1, waiting for transfers between devices, body(): lax.psum_scatter(grad_query_w, 'dp', scatter_dimension=0, tiled=True)  65.4 us
    unnamed x19, waiting for transfers between devices  65.3 us
    psum x1, waiting for transfers between devices, body(): lax.psum((grad_value_w, gain_one_grad, gain_two_grad, squares), ('dp', 't...  43.7 us
    psum x1, blocking collectives, body(): lax.psum((grad_value_w, gain_one_grad, gain_two_grad, squares), ('dp', 't...  41.1 us
    reduce_scatter x1, waiting for transfers between devices, body(): lax.psum_scatter(matmul(hidden, down_w).astype(jnp.bfloat16), 'tensor', s...  40.4 us
    reduce_scatter x1, waiting for transfers between devices, body(): lax.psum_scatter((input_part + value_input).astype(jnp.bfloat16), 'tensor...  38.3 us
  transfers between devices with their start and end apart: 18, of which 16 were waited for; matrix products, arithmetic and copies ran while one was open for 12% of the time, Pallas kernels for 0%

commit v1 on v0

--- a/solution.py
+++ b/solution.py
@@ -203,7 +203,14 @@
     resid_mid = tokens_wide + attn_out
     norm_two, normed_two, inv_two = norm_forward(resid_mid, gain_mlp)
     mlp_input = norm_two.astype(jnp.bfloat16)
-    mlp_rows = lax.all_gather(mlp_input, "tensor", axis=0, tiled=True)
+    ring = [mlp_input]
+    for hop in range(3):
+        ring.append(lax.ppermute(ring[-1], "tensor", [(dev, (dev + 1) % 4) for dev in range(4)]))
+    mlp_rows = jnp.roll(
+        jnp.concatenate(ring[::-1], axis=0),
+        (lax.axis_index("tensor") + 1) * ring[0].shape[0],
+        axis=0,
+    )
     up_pre = matmul(mlp_rows, up_w)
     hidden_act, gelu_pull = jax.vjp(gelu_tanh, up_pre)
     hidden = hidden_act.astype(jnp.bfloat16)

time: 1070 us -> 935 us (0.87)
  waiting for transfers between devices: 635 us -> 485 us
  local copies, waits for them, and re-layouts: 37.3 us -> 50.2 us
    unnamed x19 -> x18, waiting for transfers between devices: 65.3 us -> 1.31 us
    ppermute x0 -> x3, waiting for transfers between devices: none -> 41.2 us  [body(): lax.ppermute(ring[-1], 'tensor', [(dev, (dev + 1) % 4) for dev in range(4)])]
    all_gather x1 -> x0, waiting for transfers between devices: 29.1 us -> none  [body(): mlp_rows = lax.all_gather(mlp_input, 'tensor', axis=0, tiled=True)]
    reduce_scatter x1, waiting for transfers between devices: 28.7 us -> 0.01 us  [body(): lax.psum_scatter(first_part.astype(jnp.bfloat16), 'tensor', scatter_dimen...]
    all_gather x1, waiting for transfers between devices: 28.4 us -> 0.36 us  [body(): cot_rows = lax.all_gather(cotangent, 'tensor', axis=0, tiled=True)]
    reduce_scatter x1, waiting for transfers between devices: 38.3 us -> 15.2 us  [body(): lax.psum_scatter((input_part + value_input).astype(jnp.bfloat16), 'tensor...]
    all_gather x1, waiting for transfers between devices: 36.4 us -> 20.1 us  [body(): lax.all_gather(w_up, 'dp', axis=0, tiled=True)]
    unnamed x225 -> x242, local copies, waits for them, and re-layouts: 22.2 us -> 34.1 us
  transfers between devices with their start and end apart: 18 -> 20, of which waited for: 16 -> 15; matrix products, arithmetic and copies ran while one was open for 12% -> 15% of each run, Pallas kernels for 0% -> 0%
where the time goes in v1:
time: 935 us; the launch traced here: 929 us
  waiting for transfers between devices  485 us (52%)
  blocking collectives  169 us (18%)
  matrix products  140 us (15%)
  other arithmetic  63 us (7%)
  local copies, waits for them, and re-layouts  50.2 us (5%)
  between operations  18.4 us (2%)
    reduce_scatter x1, waiting for transfers between devices, body(): lax.psum_scatter(grad_down_w, 'dp', scatter_dimension=1, tiled=True)  72.2 us
    reduce_scatter x1, waiting for transfers between devices, body(): lax.psum_scatter(grad_query_w, 'dp', scatter_dimension=0, tiled=True)  65.9 us
    reduce_scatter x1, waiting for transfers between devices, body(): lax.psum_scatter(grad_key_w, 'dp', scatter_dimension=0, tiled=True)  65.4 us
    psum x1, waiting for transfers between devices, body(): lax.psum((grad_value_w, gain_one_grad, gain_two_grad, squares), ('dp', 't...  46 us
    ppermute x3, waiting for transfers between devices, body(): lax.ppermute(ring[-1], 'tensor', [(dev, (dev + 1) % 4) for dev in range(4)])  41.2 us
    psum x1, blocking collectives, body(): lax.psum((grad_value_w, gain_one_grad, gain_two_grad, squares), ('dp', 't...  41 us
    reduce_scatter x1, waiting for transfers between devices, body(): lax.psum_scatter(matmul(hidden, down_w).astype(jnp.bfloat16), 'tensor', s...  40.4 us
    reduce_scatter x1, waiting for transfers between devices, body(): lax.psum_scatter(matmul(heads_out, out_w).astype(jnp.bfloat16), 'tensor',...  36.7 us
  transfers between devices with their start and end apart: 20, of which 15 were waited for; matrix products, arithmetic and copies ran while one was open for 15% of the time, Pallas kernels for 0%

profile of v1, /device:TPU:0, one launch (start us, length us, event | category | flops | bytes accessed | tf_op | source)
XLA Modules:
  0.0 929.3 jit_solution(3441304003201086)
XLA Ops:
  16.4 32.9 %all_gather.41 = bf16[192,768]{0,1:T(8,128)(2,1)S(1)} all-gather(bf16[192,96]{0,1:T(8,128)(2,1)S(1)} %copy.36), channel_id=1, replica_groups=mesh['dp'=8,'tensor'=4] {'dp'}, dimensions={1}, use_global_device_ids=true | all-gather | bytes 331776 | tf_op jit(solution)/shard_map/all_gather | solution.py:175
  49.3 31.0 %all_gather.39 = bf16[768,192]{1,0:T(8,128)(2,1)S(1)} all-gather(bf16[96,192]{1,0:T(8,128)(2,1)S(1)} %copy-done.69), channel_id=1, replica_groups=mesh['dp'=8,'tensor'=4] {'dp'}, dimensions={0}, use_global_device_ids=true | all-gather | bytes 331776 | tf_op jit(solution)/shard_map/all_gather | solution.py:172
  80.3 31.1 %all_gather.40 = bf16[768,192]{1,0:T(8,128)(2,1)S(1)} all-gather(bf16[96,192]{1,0:T(8,128)(2,1)S(1)} %copy-done.70), channel_id=1, replica_groups=mesh['dp'=8,'tensor'=4] {'dp'}, dimensions={0}, use_global_device_ids=true | all-gather | bytes 331776 | tf_op jit(solution)/shard_map/all_gather | solution.py:173
  113.9 33.4 %all_gather.37 = bf16[768,384]{1,0:T(8,128)(2,1)} all-gather(bf16[96,384]{1,0:T(8,128)(2,1)S(1)} %copy-done.59), channel_id=1, replica_groups=mesh['dp'=8,'tensor'=4] {'dp'}, dimensions={0}, use_global_device_ids=true | all-gather | bytes 663552 | tf_op jit(solution)/shard_map/all_gather | solution.py:174
  147.3 2.4 fusion.29
  150.9 4.1 conditional.2
  151.0 3.5 fusion
  155.2 3.7 convolution_convert_fusion.5
  173.1 2.1 copy-done.1
  175.4 2.3 fusion.111
  177.8 2.6 fusion.137
  182.4 2.7 copy-done
  185.2 3.1 fusion.118
  189.0 2.8 convolution_convert_fusion.3
  193.4 36.7 %reduce-scatter.13.cloned.1.call-done = bf16[512,768]{1,0:T(8,128)(2,1)} async-done(((bf16[2048,768]{1,0:T(8,128)(2,1)}), bf16[512,768]{1,0:T(8,128)(2,1)}) %reduce-scatter.13.cloned.1.call-update) | async-done | bytes 786448 | tf_op jit(solution)/shard_map/reduce_scatter | solution.py:200
  234.2 11.4 %collective-permute-done = bf16[512,768]{1,0:T(8,128)(2,1)S(1)} collective-permute-done((bf16[512,768]{1,0:T(8,128)(2,1)S(1)}, bf16[512,768]{1,0:T(8,128)(2,1)S(1)}, u32[]{:S(2)}, u32[]{:S(2)}) %collective-permute-start) | collective-permute-done | bytes 786464 | tf_op jit(solution)/shard_map/ppermute | solution.py:208
  245.7 25.8 %collective-permute-done.1 = bf16[512,768]{1,0:T(8,128)(2,1)} collective-permute-done((bf16[512,768]{1,0:T(8,128)(2,1)S(1)}, bf16[512,768]{1,0:T(8,128)(2,1)}, u32[]{:S(2)}, u32[]{:S(2)}) %collective-permute-start.1) | collective-permute-done | bytes 786464 | tf_op jit(solution)/shard_map/ppermute | solution.py:208
  271.9 7.4 fusion.141
  279.3 3.9 collective-permute-done.2
  283.3 2.1 constant_dynamic-update-slice_fusion.7
  285.4 2.1 constant_dynamic-update-slice_fusion.6
  289.3 2.1 constant_dynamic-update-slice_fusion.3
  295.4 20.1 %all-gather.11.cloned.1.call-done = bf16[768,768]{1,0:T(8,128)(2,1)} async-done(((bf16[96,768]{1,0:T(8,128)(2,1)}), bf16[768,768]{1,0:T(8,128)(2,1)}) %all-gather.11.cloned.1.call-update) | async-done | bytes 1179664 | tf_op jit(solution)/shard_map/all_gather | solution.py:176
  315.5 11.2 %fusion.17 = (bf16[2048,768]{1,0:T(8,128)(2,1)S(1)}, f32[2048,768]{1,0:T(8,128)}) fusion(f32[2048,768]{1,0:T(8,128)} %fusion.141, bf16[768,768]{1,0:T(8,128)(2,1)} %all-gather.11.cloned.1.call-done, bf16[4096,768]{1,0:T(8,128)(2,1)} %constant_dynamic-update-slice_fusion, s32[]{:T(128)S(6)} %select_n.58), kind=kOutput, calls=%fused_computation.35 | convolution fusion | flops 2447376384 | bytes 20054020 | tf_op jit(solution)/shard_map/dot_general | solution.py:13
  328.4 4.1 convolution_convert_fusion.1
  333.7 8.4 convolution_convert_fusion.2
  342.2 26.7 %reduce-scatter.17.cloned.1.call-done = bf16[512,768]{1,0:T(8,128)(2,1)} async-done(((bf16[2048,768]{1,0:T(8,128)(2,1)}), bf16[512,768]{1,0:T(8,128)(2,1)}) %reduce-scatter.17.cloned.1.call-update) | async-done | bytes 786448 | tf_op jit(solution)/shard_map/reduce_scatter | solution.py:243
  368.9 40.4 %reduce-scatter.15.cloned.1.call-done = bf16[512,768]{1,0:T(8,128)(2,1)} async-done(((bf16[2048,768]{1,0:T(8,128)(2,1)}), bf16[512,768]{1,0:T(8,128)(2,1)}) %reduce-scatter.15.cloned.1.call-update) | async-done | bytes 786448 | tf_op jit(solution)/shard_map/reduce_scatter | solution.py:217
  409.3 4.5 fusion.84
  413.9 3.1 fusion.132
  417.4 28.3 %all-gather.17.cloned.1.call-done = bf16[2048,768]{1,0:T(8,128)(2,1)} async-done(((bf16[512,768]{1,0:T(8,128)(2,1)}), bf16[2048,768]{1,0:T(8,128)(2,1)}) %all-gather.17.cloned.1.call-update) | async-done | bytes 3145744 | tf_op jit(solution)/shard_map/all_gather | solution.py:248
  445.7 3.2 convolution_convert_fusion.4
  449.9 2.9 multiply_reduce_fusion.3
  453.0 8.9 multiply_reduce_fusion.1
  463.2 2.1 fusion.55
  466.3 2.2 fusion.58
  468.5 16.6 %conditional.3 = (f32[768,384]{0,1:T(8,128)}, bf16[2048,384]{1,0:T(8,128)(2,1)S(1)}, f32[2048,768]{1,0:T(8,128)}) conditional(s32[]{:T(128)} %convert_element_type.169, (s32[]{:T(128)}, bf16[2048,192]{0,1:T(8,128)(2,1)S(1)}) %tuple.157, (bf16[2048,192]{0,1:T(8,128)(2,1)S(1)}, bf16[2048,768]{1,0:T(8,128)(2,1)}, s32[]{:T(128)}, ...), branch_computations={%region_23.24_spmd, %region_24.25_spmd} | conditional | flops 1207959552 | bytes 28901462 | solution.py:286
  470.2 3.6 convolution_dynamic-update-slice_fusion
  473.7 4.7 convolution_bitcast_fusion
  478.4 6.5 copy.51
  485.1 3.2 copy.43
  488.6 7.4 multiply_convert_fusion.1
  496.1 2.2 copy-done.6
  498.4 2.2 fusion.122
  500.6 2.2 convolution_bitcast_fusion.1
  502.9 5.5 multiply_reduce_fusion.2
  508.5 3.9 multiply_convert_fusion.4
  513.2 3.9 multiply_convert_fusion.2
  520.6 6.5 multiply_reduce_fusion
  527.5 9.6 %multiply_convert_fusion = bf16[3,512,2048]{2,1,0:T(8,128)(2,1)S(1)} fusion(f32[3,512,2048]{2,1,0:T(8,128)} %get-tuple-element.261, f32[3,512,2048]{2,1,0:T(8,128)} %copy-done, f32[3,512]{1,0:T(4,128)S(1)} %get-tuple-element.260, f32[3,512]{1,0:T(4,128)S(1)} %log_add_fusion), kind=kLoop, calls=%fused_computation.11 | loop fusion | flops 12582912 | bytes 31469568 | tf_op jit(solution)/shard_map/convert_element_type | solution.py:127
  546.0 5.7 add_convert_fusion
  551.8 7.0 fusion.37
  559.0 8.4 fusion.133
  567.5 3.8 fusion.144
  572.0 2.7 pad_maximum_fusion.4
  574.7 3.8 fusion.143
  578.6 46.0 %all-reduce.5.cloned.1.call-done = f32[768,384]{1,0:T(8,128)} async-done(((f32[768,384]{1,0:T(8,128)}), f32[768,384]{1,0:T(8,128)}) %all-reduce.5.cloned.1.call-update) | async-done | bytes 1179664 | tf_op jit(solution)/shard_map/psum | solution.py:309
  629.8 15.2 %reduce-scatter.19.cloned.1.call-done = bf16[512,768]{1,0:T(8,128)(2,1)} async-done(((bf16[2048,768]{1,0:T(8,128)(2,1)}), bf16[512,768]{1,0:T(8,128)(2,1)}) %reduce-scatter.19.cloned.1.call-update) | async-done | bytes 786448 | tf_op jit(solution)/shard_map/reduce_scatter | solution.py:290
  647.0 41.0 %all-reduce.2 = (f32[768]{0:T(1024)}, f32[768]{0:T(1024)}, f32[4]{0:T(128)S(1)}) all-reduce(f32[768]{0:T(1024)S(1)} %get-tuple-element.223, f32[768]{0:T(1024)S(1)} %copy-done.91, f32[4]{0:T(128)S(1)} %pad_maximum_fusion.4), channel_id=1, replica_groups=mesh['dp'=8,'tensor'=4] {'dp','tensor'}, use_global_device_ids=true, to_apply=%region_36.37 | all-reduce | flops 1540 | bytes 12320 | tf_op jit(solution)/shard_map/psum | solution.py:309
  689.8 3.2 fusion.78
  693.0 25.5 %reduce-scatter.27.cloned.1.call-done = f32[96,768]{1,0:T(8,128)} async-done(((f32[768,768]{1,0:T(8,128)}), f32[96,768]{1,0:T(8,128)}) %reduce-scatter.27.cloned.1.call-update) | async-done | bytes 294928 | tf_op jit(solution)/shard_map/reduce_scatter | solution.py:306
  718.5 72.2 %reduce-scatter.29.cloned.1.call-done = f32[768,96]{0,1:T(8,128)} async-done(((f32[768,768]{0,1:T(8,128)}), f32[768,96]{0,1:T(8,128)}) %reduce-scatter.29.cloned.1.call-update) | async-done | bytes 294928 | tf_op jit(solution)/shard_map/reduce_scatter | solution.py:307
  790.7 65.4 %reduce-scatter.25.cloned.1.call-done = f32[96,192]{1,0:T(8,128)} async-done(((f32[768,192]{1,0:T(8,128)}), f32[96,192]{1,0:T(8,128)}) %reduce-scatter.25.cloned.1.call-update) | async-done | bytes 73744 | tf_op jit(solution)/shard_map/reduce_scatter | solution.py:304
  856.1 65.9 %reduce-scatter.23.cloned.1.call-done = f32[96,192]{1,0:T(8,128)} async-done(((f32[768,192]{1,0:T(8,128)}), f32[96,192]{1,0:T(8,128)}) %reduce-scatter.23.cloned.1.call-update) | async-done | bytes 73744 | tf_op jit(solution)/shard_map/reduce_scatter | solution.py:303
  (357 shorter events, 71.9 us)
Async XLA Ops:
  8.0 41.3 %copy-start.69 = (bf16[96,192]{1,0:T(8,128)(2,1)S(1)}, bf16[96,192]{1,0:T(8,128)(2,1)}, u32[]{:S(2)}) copy-start(bf16[96,192]{1,0:T(8,128)(2,1)} %param.41) | copy-start | bytes 110596
  8.0 72.2 %copy-start.70 = (bf16[96,192]{1,0:T(8,128)(2,1)S(1)}, bf16[96,192]{1,0:T(8,128)(2,1)}, u32[]{:S(2)}) copy-start(bf16[96,192]{1,0:T(8,128)(2,1)} %param.42) | copy-start | bytes 110596
  8.1 142.8 %all-gather.7.cloned.1.call-start = ((), (), s32[]{:S(2)}) async-start(), calls=%async_computation.10 | async-start | bytes 1966080 | tf_op jit(solution)/shard_map/all_gather | solution.py:184
  8.1 103.2 %copy-start.50 = (s32[2048]{0:T(1024)S(1)}, s32[2048]{0:T(1024)}, u32[]{:S(2)}) copy-start(s32[2048]{0:T(1024)} %param.39) | copy-start | bytes 24580
  10.1 102.3 %slice-start.13 = ((s32[2048]{0:T(1024)}), s32[1024]{0:T(1024)S(1)}, s32[]{:S(2)}) async-start(s32[2048]{0:T(1024)} %param.39), calls=%async_computation.40 | async-start | bytes 8192 | tf_op jit(solution)/shard_map/slice | solution.py:49
  10.1 103.8 %copy-start.59 = (bf16[96,384]{1,0:T(8,128)(2,1)S(1)}, bf16[96,384]{1,0:T(8,128)(2,1)}, u32[]{:S(2)}) copy-start(bf16[96,384]{1,0:T(8,128)(2,1)} %param.43) | copy-start | bytes 221188
  10.1 140.8 %all-gather.9.cloned.1.call-start = ((), (), s32[]{:S(2)}) async-start(), calls=%async_computation.11 | async-start | bytes 3932160 | tf_op jit(solution)/shard_map/all_gather | solution.py:183
  15.5 214.6 %reduce-scatter.13.cloned.1.call-start = ((), (), s32[]{:S(2)}) async-start(), calls=%async_computation.12 | async-start | bytes 3932160 | tf_op jit(solution)/shard_map/reduce_scatter | solution.py:200
  80.3 78.7 %copy-start.23 = (bf16[768,192]{1,0:T(8,128)(2,1)}, bf16[768,192]{1,0:T(8,128)(2,1)S(1)}, u32[]{:S(2)}) copy-start(bf16[768,192]{1,0:T(8,128)(2,1)S(1)} %all_gather.39) | copy-start | bytes 884740
  111.3 43.8 %copy-start.27 = (bf16[768,192]{1,0:T(8,128)(2,1)}, bf16[768,192]{1,0:T(8,128)(2,1)S(1)}, u32[]{:S(2)}) copy-start(bf16[768,192]{1,0:T(8,128)(2,1)S(1)} %all_gather.40) | copy-start | bytes 884740
  155.0 27.4 %copy-start.13 = (bf16[2048,192]{0,1:T(8,128)(2,1)}, bf16[2048,192]{0,1:T(8,128)(2,1)S(1)}, u32[]{:S(2)}) copy-start(bf16[2048,192]{0,1:T(8,128)(2,1)S(1)} %get-tuple-element.276) | copy-start | bytes 2359300
  155.1 11.5 %copy-start.41 = (bf16[1024,192]{0,1:T(8,128)(2,1)}, bf16[1024,192]{0,1:T(8,128)(2,1)S(1)}, u32[]{:S(2)}) copy-start(bf16[1024,192]{0,1:T(8,128)(2,1)S(1)} %slice.378) | copy-start | bytes 1179652
  155.2 18.0 %copy-start.30 = (bf16[1536,192]{0,1:T(8,128)(2,1)}, bf16[1536,192]{0,1:T(8,128)(2,1)S(1)}, u32[]{:S(2)}) copy-start(bf16[1536,192]{0,1:T(8,128)(2,1)S(1)} %slice.381) | copy-start | bytes 1769476
  158.9 18.9 %copy-start.15 = (bf16[2048,192]{0,1:T(8,128)(2,1)}, bf16[2048,192]{0,1:T(8,128)(2,1)S(1)}, u32[]{:S(2)}) copy-start(bf16[2048,192]{0,1:T(8,128)(2,1)S(1)} %convolution_convert_fusion.5) | copy-start | bytes 2359300
  159.0 10.6 %copy-start.21 = (bf16[1536,192]{0,1:T(8,128)(2,1)}, bf16[1536,192]{0,1:T(8,128)(2,1)S(1)}, u32[]{:S(2)}) copy-start(bf16[1536,192]{0,1:T(8,128)(2,1)S(1)} %slice.383) | copy-start | bytes 1769476
  169.6 18.7 %copy-start.96 = (bf16[3,64,512]{2,1,0:T(8,128)(2,1)}, bf16[3,64,512]{2,1,0:T(8,128)(2,1)S(1)}, u32[]{:S(2)}) copy-start(bf16[3,64,512]{2,1,0:T(8,128)(2,1)S(1)} %fusion.117) | copy-start | bytes 589828
  177.8 10.6 %copy-start.98 = (bf16[3,64,512]{2,1,0:T(8,128)(2,1)}, bf16[3,64,512]{2,1,0:T(8,128)(2,1)S(1)}, u32[]{:S(2)}) copy-start(bf16[3,64,512]{2,1,0:T(8,128)(2,1)S(1)} %fusion.111) | copy-start | bytes 589828
  191.8 42.0 %copy-start.62 = (f32[768]{0:T(1024)S(1)}, f32[768]{0:T(1024)}, u32[]{:S(2)}) copy-start(f32[768]{0:T(1024)} %param.48) | copy-start | bytes 9220
  191.8 79.7 %all-gather.13.cloned.1.call-start = ((), (), s32[]{:S(2)}) async-start(), calls=%async_computation.14 | async-start | bytes 1327104 | tf_op jit(solution)/shard_map/all_gather | solution.py:177
  192.4 79.5 %all-gather.15.cloned.1.call-start = ((), (), s32[]{:S(2)}) async-start(), calls=%async_computation.16 | async-start | bytes 3932160 | tf_op jit(solution)/shard_map/all_gather | solution.py:238
  193.0 122.5 %all-gather.11.cloned.1.call-start = ((), (), s32[]{:S(2)}) async-start(), calls=%async_computation.13 | async-start | bytes 1327104 | tf_op jit(solution)/shard_map/all_gather | solution.py:176
  231.6 182.2 %copy-start.55 = (f32[512]{0:T(512)}, f32[512]{0:T(512)S(1)}, u32[]{:S(2)}) copy-start(f32[512]{0:T(512)S(1)} %broadcast_multiply_fusion.4) | copy-start | bytes 6148
  234.1 11.5 %collective-permute-start = (bf16[512,768]{1,0:T(8,128)(2,1)S(1)}, bf16[512,768]{1,0:T(8,128)(2,1)S(1)}, u32[]{:S(2)}, u32[]{:S(2)}) collective-permute-start(bf16[512,768]{1,0:T(8,128)(2,1)S(1)} %multiply_convert_fusion.5), channel_id=1, source_target_pairs={{0,1},{1,2},{2,3},{3,0},{4,5},{5,6},{6,7},{7,4},{8,9},{9,10},{10,1... | collective-permute-start | bytes 2359304 | tf_op jit(solution)/shard_map/ppermute | solution.py:208
  245.6 25.9 %collective-permute-start.1 = (bf16[512,768]{1,0:T(8,128)(2,1)S(1)}, bf16[512,768]{1,0:T(8,128)(2,1)}, u32[]{:S(2)}, u32[]{:S(2)}) collective-permute-start(bf16[512,768]{1,0:T(8,128)(2,1)S(1)} %collective-permute-done), channel_id=1, source_target_pairs={{0,1},{1,2},{2,3},{3,0},{4,5},{5,6},{6,7},{7,4},{8,9},{9,10},{10,1... | collective-permute-start | bytes 2359304 | tf_op jit(solution)/shard_map/ppermute | solution.py:208
  245.6 123.2 %reduce-scatter.17.cloned.1.call-start = ((), (), s32[]{:S(2)}) async-start(), calls=%async_computation.17 | async-start | bytes 3932160 | tf_op jit(solution)/shard_map/reduce_scatter | solution.py:243
  271.5 11.7 %collective-permute-start.2 = (bf16[512,768]{1,0:T(8,128)(2,1)}, bf16[512,768]{1,0:T(8,128)(2,1)}, u32[]{:S(2)}, u32[]{:S(2)}) collective-permute-start(bf16[512,768]{1,0:T(8,128)(2,1)} %collective-permute-done.1), channel_id=1, source_target_pairs={{0,1},{1,2},{2,3},{3,0},{4,5},{5,6},{6,7},{7,4},{8,9},{9,10},{10,1... | collective-permute-start | bytes 2359304 | tf_op jit(solution)/shard_map/ppermute | solution.py:208
  315.5 12.8 %copy-start.93 = (bf16[768,768]{1,0:T(8,128)(2,1)S(1)}, bf16[768,768]{1,0:T(8,128)(2,1)}, u32[]{:S(2)}) copy-start(bf16[768,768]{1,0:T(8,128)(2,1)} %all-gather.11.cloned.1.call-done) | copy-start | bytes 3538948
  332.5 76.8 %reduce-scatter.15.cloned.1.call-start = ((), (), s32[]{:S(2)}) async-start(), calls=%async_computation.15 | async-start | bytes 3932160 | tf_op jit(solution)/shard_map/reduce_scatter | solution.py:217
  342.1 67.1 %copy-start.67 = (f32[512]{0:T(512)S(1)}, f32[512]{0:T(512)}, u32[]{:S(2)}) copy-start(f32[512]{0:T(512)} %copy-done.66) | copy-start | bytes 6148
  342.1 103.6 %all-gather.17.cloned.1.call-start = ((), (), s32[]{:S(2)}) async-start(), calls=%async_computation.18 | async-start | bytes 3932160 | tf_op jit(solution)/shard_map/all_gather | solution.py:248
  413.8 31.9 %copy-start.89 = (f32[512]{0:T(512)}, f32[512]{0:T(512)S(1)}, u32[]{:S(2)}) copy-start(f32[512]{0:T(512)S(1)} %get-tuple-element.269) | copy-start | bytes 6148
  413.8 35.1 %copy-start.87 = (f32[512]{0:T(512)}, f32[512]{0:T(512)S(1)}, u32[]{:S(2)}) copy-start(f32[512]{0:T(512)S(1)} %get-tuple-element.268) | copy-start | bytes 6148
  413.8 48.1 %slice-start.9 = ((s8[6291456]{0:T(1024)(128)(4,1)}), s8[2097152]{0:T(1024)(128)(4,1)S(1)}, s32[]{:S(2)}) async-start(s8[6291456]{0:T(1024)(128)(4,1)} %bitcast.171), calls=%async_computation.36 | async-start | bytes 4194304
  417.0 207.5 %all-reduce.5.cloned.1.call-start = ((), (), s32[]{:S(2)}) async-start(), calls=%async_computation.23 | async-start | bytes 2359296 | tf_op jit(solution)/shard_map/psum | solution.py:309
  417.3 32.4 %copy-start.53 = (f32[3,512]{1,0:T(4,128)}, f32[3,512]{1,0:T(4,128)S(1)}, u32[]{:S(2)}) copy-start(f32[3,512]{1,0:T(4,128)S(1)} %log_add_fusion.3) | copy-start | bytes 18436
  417.3 44.6 %copy-start.51 = (f32[3,512]{1,0:T(4,128)}, f32[3,512]{1,0:T(4,128)S(1)}, u32[]{:S(2)}) copy-start(f32[3,512]{1,0:T(4,128)S(1)} %log_add_fusion.2) | copy-start | bytes 18436
  449.9 13.3 %slice-start.6 = ((s8[9437184]{0:T(1024)(128)(4,1)}), s8[4194304]{0:T(1024)(128)(4,1)S(1)}, s32[]{:S(2)}) async-start(s8[9437184]{0:T(1024)(128)(4,1)} %bitcast.169), calls=%async_computation.33 | async-start | bytes 8388608
  453.0 10.2 %slice-start.7 = ((s8[9437184]{0:T(1024)(128)(4,1)}), s8[4194304]{0:T(1024)(128)(4,1)S(1)}, s32[]{:S(2)}) async-start(s8[9437184]{0:T(1024)(128)(4,1)} %bitcast.169), calls=%async_computation.34 | async-start | bytes 8388608
  453.0 10.2 %slice-start.8 = ((s8[9437184]{0:T(1024)(128)(4,1)}), s8[1048576]{0:T(1024)(128)(4,1)S(1)}, s32[]{:S(2)}) async-start(s8[9437184]{0:T(1024)(128)(4,1)} %bitcast.169), calls=%async_computation.35 | async-start | bytes 2097152
  453.0 12.3 %slice-start = ((s8[12582912]{0:T(1024)(128)(4,1)}), s8[4194304]{0:T(1024)(128)(4,1)S(1)}, s32[]{:S(2)}) async-start(s8[12582912]{0:T(1024)(128)(4,1)} %bitcast.165), calls=%async_computation.27 | async-start | bytes 8388608
  453.0 12.3 %slice-start.1 = ((s8[12582912]{0:T(1024)(128)(4,1)}), s8[4194304]{0:T(1024)(128)(4,1)S(1)}, s32[]{:S(2)}) async-start(s8[12582912]{0:T(1024)(128)(4,1)} %bitcast.165), calls=%async_computation.28 | async-start | bytes 8388608
  485.1 11.0 %copy-start.20 = (bf16[2048,384]{1,0:T(8,128)(2,1)}, bf16[2048,384]{1,0:T(8,128)(2,1)S(1)}, u32[]{:S(2)}) copy-start(bf16[2048,384]{1,0:T(8,128)(2,1)S(1)} %get-tuple-element.206) | copy-start | bytes 4718596
  488.4 137.8 %reduce-scatter.31.cloned.1.call-start = ((), (), s32[]{:S(2)}) async-start(), calls=%async_computation.26 | async-start | bytes 884736
  488.6 9.7 %copy-start.22 = (bf16[1536,192]{0,1:T(8,128)(2,1)S(1)}, bf16[1536,192]{0,1:T(8,128)(2,1)}, u32[]{:S(2)}) copy-start(bf16[1536,192]{0,1:T(8,128)(2,1)} %copy-done.21) | copy-start | bytes 1769476
  508.4 119.4 %reduce-scatter.21.cloned.1.call-start = ((), (), s32[]{:S(2)}) async-start(), calls=%async_computation.20 | async-start | bytes 1966080 | tf_op jit(solution)/shard_map/reduce_scatter | solution.py:296
  508.5 12.0 %slice-start.3 = ((s8[12582912]{0:T(1024)(128)(4,1)}), s8[4194304]{0:T(1024)(128)(4,1)S(1)}, s32[]{:S(2)}) async-start(s8[12582912]{0:T(1024)(128)(4,1)} %bitcast.167), calls=%async_computation.30 | async-start | bytes 8388608
  527.1 117.9 %reduce-scatter.19.cloned.1.call-start = ((), (), s32[]{:S(2)}) async-start(), calls=%async_computation.19 | async-start | bytes 3932160 | tf_op jit(solution)/shard_map/reduce_scatter | solution.py:290
  527.5 9.6 %copy-start.40 = (bf16[512,192]{0,1:T(8,128)(2,1)S(1)}, bf16[512,192]{0,1:T(8,128)(2,1)}, u32[]{:S(2)}) copy-start(bf16[512,192]{0,1:T(8,128)(2,1)} %copy-done.39) | copy-start | bytes 589828
  551.7 166.8 %reduce-scatter.27.cloned.1.call-start = ((), (), s32[]{:S(2)}) async-start(), calls=%async_computation.24 | async-start | bytes 2654208 | tf_op jit(solution)/shard_map/reduce_scatter | solution.py:306
  558.8 231.9 %reduce-scatter.29.cloned.1.call-start = ((), (), s32[]{:S(2)}) async-start(), calls=%async_computation.25 | async-start | bytes 2654208 | tf_op jit(solution)/shard_map/reduce_scatter | solution.py:307
  567.5 288.7 %reduce-scatter.25.cloned.1.call-start = ((), (), s32[]{:S(2)}) async-start(), calls=%async_computation.22 | async-start | bytes 884736 | tf_op jit(solution)/shard_map/reduce_scatter | solution.py:304
  571.3 350.7 %reduce-scatter.23.cloned.1.call-start = ((), (), s32[]{:S(2)}) async-start(), calls=%async_computation.21 | async-start | bytes 884736 | tf_op jit(solution)/shard_map/reduce_scatter | solution.py:303
  574.7 70.3 %copy-start.65 = (f32[512]{0:T(512)S(1)}, f32[512]{0:T(512)}, u32[]{:S(2)}) copy-start(f32[512]{0:T(512)} %copy-done.64) | copy-start | bytes 6148
  574.7 70.3 %copy-start.72 = (f32[768]{0:T(1024)S(1)}, f32[768]{0:T(1024)}, u32[]{:S(2)}) copy-start(f32[768]{0:T(1024)} %param.47) | copy-start | bytes 9220
  574.7 70.3 %copy-start.75 = (f32[512]{0:T(512)S(1)}, f32[512]{0:T(512)}, u32[]{:S(2)}) copy-start(f32[512]{0:T(512)} %copy-done.74) | copy-start | bytes 6148
  578.5 68.5 %copy-start.91 = (f32[768]{0:T(1024)S(1)}, f32[768]{0:T(1024)}, u32[]{:S(2)}) copy-start(f32[768]{0:T(1024)} %get-tuple-element.221) | copy-start | bytes 9220
  578.5 111.2 %copy-start.11 = (bf16[512,768]{1,0:T(8,128)(2,1)S(1)}, bf16[512,768]{1,0:T(8,128)(2,1)}, u32[]{:S(2)}) copy-start(bf16[512,768]{1,0:T(8,128)(2,1)} %reduce-scatter.13.cloned.1.call-done) | copy-start | bytes 2359300
  578.5 111.2 %copy-start.17 = (bf16[512,768]{1,0:T(8,128)(2,1)S(1)}, bf16[512,768]{1,0:T(8,128)(2,1)}, u32[]{:S(2)}) copy-start(bf16[512,768]{1,0:T(8,128)(2,1)} %param.49) | copy-start | bytes 2359300
  578.5 111.2 %copy-start.19 = (bf16[512,768]{1,0:T(8,128)(2,1)S(1)}, bf16[512,768]{1,0:T(8,128)(2,1)}, u32[]{:S(2)}) copy-start(bf16[512,768]{1,0:T(8,128)(2,1)} %reduce-scatter.17.cloned.1.call-done) | copy-start | bytes 2359300
  578.5 111.2 %copy-start.56 = (f32[512]{0:T(512)S(1)}, f32[512]{0:T(512)}, u32[]{:S(2)}) copy-start(f32[512]{0:T(512)} %copy-done.55) | copy-start | bytes 6148
  578.5 111.2 %copy-start.63 = (f32[768]{0:T(1024)S(1)}, f32[768]{0:T(1024)}, u32[]{:S(2)}) copy-start(f32[768]{0:T(1024)} %param.48) | copy-start | bytes 9220
  578.5 111.2 %copy-start.68 = (f32[512]{0:T(512)S(1)}, f32[512]{0:T(512)}, u32[]{:S(2)}) copy-start(f32[512]{0:T(512)} %copy-done.66) | copy-start | bytes 6148
  578.6 111.2 %copy-start.88 = (f32[512]{0:T(512)S(1)}, f32[512]{0:T(512)}, u32[]{:S(2)}) copy-start(f32[512]{0:T(512)} %copy-done.87) | copy-start | bytes 6148
  578.6 111.2 %copy-start.90 = (f32[512]{0:T(512)S(1)}, f32[512]{0:T(512)}, u32[]{:S(2)}) copy-start(f32[512]{0:T(512)} %copy-done.89) | copy-start | bytes 6148
  (73 other events, 235.5 us)
Sparse Core Ops, SparseCore 0:
  10.4 22.3 all-gather.6
  35.0 28.5 all-gather.8
  191.9 38.1 reduce-scatter.12
  417.1 28.5 all-gather.16
  488.5 136.0 all-reduce.4
Sparse Core Ops, SparseCore 1:
  194.5 41.7 all-gather.12
  237.6 34.2 all-gather.14
  274.0 41.5 all-gather.10
  332.6 36.2 reduce-scatter.16
  371.4 37.8 reduce-scatter.14
  508.5 65.6 reduce-scatter.30
  577.1 27.4 reduce-scatter.20
  607.1 37.8 reduce-scatter.18
  648.9 69.5 reduce-scatter.26
  722.6 68.0 reduce-scatter.28
  794.4 61.6 reduce-scatter.24
  860.4 61.6 reduce-scatter.22
